TPU v7x, 32 devices: a whole 2x2x4 slice. The times are simulated.
32 devices in a mesh: groups: 2 (over y), seq: 4 (over z), head: 2 (over x), batch: 2 (over core).
Axes of the slice: x: 2, y: 2, z: 4, core: 2. Of those that a mesh axis runs over, the one named last changes fastest.
Arguments:
- queries: bfloat16 [4, 512, 2560], P(('groups', 'batch'), 'seq', 'head'), parts along dimension 0, may hold values from -6 to 6
- keys: bfloat16 [4, 512, 2560], P(('groups', 'batch'), 'seq', 'head'), parts along dimension 0, may hold values from -6 to 6
- values: bfloat16 [4, 512, 2560], P(('groups', 'batch'), 'seq', 'head'), parts along dimension 0, may hold values from -6 to 6
- cache_keys: bfloat16 [4, 8, 32, 2560], P(('groups', 'batch'), 'seq', None, 'head'), parts along dimension 0, may hold values from -6 to 6
- cache_values: bfloat16 [4, 8, 32, 2560], P(('groups', 'batch'), 'seq', None, 'head'), parts along dimension 0, may hold values from -6 to 6
- frame_list: int32 [4, 3], P(('groups', 'batch')), parts along dimension 0, may hold values from 0 to 7, as said below
- frame_place: int32 [4, 8], P(('groups', 'batch')), parts along dimension 0, may hold values from 0 to 7, each once within a row
- tile_mask: int32 [4, 4, 4], P(('groups', 'batch'), 'seq'), parts along dimension 0, may hold values from 0 to 1, as said below
Outputs:
- attention: bfloat16 [4, 512, 2560], P(('groups', 'batch'), 'seq', 'head'), parts along dimension 0
There are 2 independent parts, one for each index of `groups`. A program takes and returns all parts, laid end to end along the dimension named above; each array names one. Nothing has to cross between parts.
Inputs may be any that keep to these rules, and one draw needn't show every extreme that they name: `frame_list`: each row holds frame 0 and then 3 - 1 consecutive frame numbers. `tile_mask`: ones on the diagonal of each video's tile matrix.
All inputs are finite; a program needn't handle non-finite values.
Results may differ from a plain program's by a relative error of at most 0.006.
Values may be sent and summed in bfloat16 or wider, within the bound.
No kernel may reach another device: no remote copies, remote signals or barrier semaphores. Data moves between devices by JAX's collectives and lax.ppermute only.
A program may use at most 128 MiB of HBM per device.

v0:
```python
import math
import jax
import jax.numpy as jnp
from jax import lax
from jax.sharding import PartitionSpec as P

HD = 128
TILE = 128
NEG_FILL = -1e30


def attend(running, key_part, value_part, live, query_heads):
    videos, length, col_count = key_part.shape
    head_count = col_count // HD

    def update(previous):
        peak_old, total_old, summed_old = previous
        key_heads = key_part.reshape(videos, length, head_count, HD)
        value_heads = value_part.reshape(videos, length, head_count, HD)
        scores = jnp.einsum(
            "vqhd,vkhd->vhqk", query_heads, key_heads, preferred_element_type=jnp.float32
        ) * (1.0 / math.sqrt(HD))
        allowed = live[:, None, :, :]
        scores = jnp.where(allowed, scores, NEG_FILL)
        peak_new = jnp.maximum(peak_old, jnp.max(scores, axis=3))
        weights = jnp.where(allowed, jnp.exp(scores - peak_new[..., None]), 0.0)
        factor = jnp.exp(peak_old - peak_new)
        total_new = total_old * factor + jnp.sum(weights, axis=3)
        product = jnp.einsum(
            "vhqk,vkhd->vhqd",
            weights.astype(jnp.bfloat16),
            value_heads,
            preferred_element_type=jnp.float32,
        )
        summed_new = summed_old * factor[..., None] + product
        return (peak_new, total_new, summed_new)

    def unchanged(previous):
        return previous

    return lax.cond(jnp.any(live), update, unchanged, running)


def body(queries, keys, values, cache_keys, cache_values, frame_list, frame_place, tile_mask):
    videos, tok_rows, col_count = queries.shape
    head_count = col_count // HD
    query_heads = queries.reshape(videos, tok_rows, head_count, HD)
    running = (
        jnp.full((videos, head_count, tok_rows), NEG_FILL, jnp.float32),
        jnp.zeros((videos, head_count, tok_rows), jnp.float32),
        jnp.zeros((videos, head_count, tok_rows, HD), jnp.float32),
    )
    frame_tok = cache_keys.shape[2]
    listed = jnp.any(frame_place[:, :, None] == frame_list[:, None, :], axis=2)
    key_piece = lax.all_gather(cache_keys, "seq", axis=1, tiled=True)
    value_piece = lax.all_gather(cache_values, "seq", axis=1, tiled=True)
    count_frames = key_piece.shape[1]
    token_flags = jnp.repeat(listed, frame_tok, axis=1)
    live = jnp.broadcast_to(token_flags[:, None, :], (videos, tok_rows, count_frames * frame_tok))
    key_flat = key_piece.reshape(videos, count_frames * frame_tok, col_count)
    value_flat = value_piece.reshape(videos, count_frames * frame_tok, col_count)
    running = attend(running, key_flat, value_flat, live, query_heads)
    key_piece = lax.all_gather(keys, "seq", axis=1, tiled=True)
    value_piece = lax.all_gather(values, "seq", axis=1, tiled=True)
    length = key_piece.shape[1]
    key_tiles = jnp.arange(length, dtype=jnp.int32) // TILE
    tile_live = jnp.take(tile_mask, key_tiles, axis=2)
    running = attend(
        running, key_piece, value_piece, jnp.repeat(tile_live, TILE, axis=1) > 0, query_heads
    )
    peak, total, summed = running
    result = summed / total[..., None]
    return result.transpose(0, 2, 1, 3).reshape(videos, tok_rows, col_count).astype(jnp.bfloat16)


def solution(mesh):
    return jax.shard_map(
        body,
        mesh=mesh,
        in_specs=(
            P(("groups", "batch"), "seq", "head"),
            P(("groups", "batch"), "seq", "head"),
            P(("groups", "batch"), "seq", "head"),
            P(("groups", "batch"), "seq", None, "head"),
            P(("groups", "batch"), "seq", None, "head"),
            P(("groups", "batch"), None),
            P(("groups", "batch"), None),
            P(("groups", "batch"), "seq", None),
        ),
        out_specs=P(("groups", "batch"), "seq", "head"),
        check_vma=False,
    )
```

profile of v0, /device:TPU:0, one launch (start us, length us, event | category | flops | bytes accessed | tf_op | source)
XLA Modules:
  0.0 110.2 jit_solution(18014833076720647111)
XLA Ops:
  6.6 1.9 %copy.50 = bf16[1,128,1280]{1,2,0:T(8,128)(2,1)} copy(bf16[1,128,1280]{2,1,0:T(8,128)(2,1)} %param.13) | data formatting | bytes 655360 | tf_op args[1]
  8.6 1.9 %copy.51 = bf16[1,128,1280]{1,2,0:T(8,128)(2,1)} copy(bf16[1,128,1280]{2,1,0:T(8,128)(2,1)} %param.14) | data formatting | bytes 655360 | tf_op args[2]
  10.6 0.7 fusion.41
  11.2 2.7 %compare_select_fusion.1 = s32[512,1]{0,1:T(1,128)S(1)} fusion(s32[]{:T(128)} %bitcast.15, s32[]{:T(128)} %bitcast.16, s32[]{:T(128)} %bitcast.18, s32[]{:T(128)} %bitcast.17), kind=kLoop, calls=%fused_computation.45 | loop fusion | flops 8704 | bytes 2064 | tf_op jit(solution)/shard_map/jit(_take)/gather | solution.py:67
  14.0 0.8 broadcast_reduce_fusion
  15.6 0.1 broadcast_in_dim.89
  15.7 0.7 broadcast_reduce_fusion.1
  17.2 0.2 copy.44
  17.4 27.2 %all_gather.12 = bf16[1,8,32,1280]{3,2,0,1:T(8,128)(2,1)S(1)} all-gather(bf16[1,2,32,1280]{3,2,0,1:T(8,128)(2,1)S(1)} %bitcast.73), channel_id=1, replica_groups=mesh['groups'=2,'seq'=4,'head'=2,'batch'=2] {'seq'}, dimensions={1}, use_global_device_ids=true | all-gather | bytes 819200 | tf_op jit(solution)/shard_map/all_gather | solution.py:55
  44.6 21.8 %all_gather.13 = bf16[1,8,32,1280]{3,2,0,1:T(8,128)(2,1)S(1)} all-gather(bf16[1,2,32,1280]{3,2,0,1:T(8,128)(2,1)S(1)} %bitcast.74), channel_id=1, replica_groups=mesh['groups'=2,'seq'=4,'head'=2,'batch'=2] {'seq'}, dimensions={1}, use_global_device_ids=true | all-gather | bytes 819200 | tf_op jit(solution)/shard_map/all_gather | solution.py:56
  66.3 3.3 %conditional.2 = (f32[1,10,128]{2,1,0:T(8,128)S(1)}, f32[1,10,128]{2,1,0:T(8,128)S(1)}, f32[1,10,128,128]{3,2,1,0:T(8,128)}) conditional(s32[]{:T(128)} %convert_element_type.32, () %tuple.20, (pred[8]{0:T(512)(128)(4,1)S(1)}, bf16[1,128,10,128]{1,3,2,0:T(8,128)(2,1)S(1)}, bf16[1,8,32,1280]{3,2,0,1:T(8,128)(2,1)S(1)}, ...), branch_computations={%region_3.4_spmd, %region_4.7_spmd} | conditional | flops 170891520 | bytes 8910368 | solution.py:41
  66.3 0.4 reshape.260
  66.9 0.5 fusion.40
  67.4 0.5 fusion.3
  67.9 0.4 reshape.261
  68.3 1.3 %fusion.1 = f32[1,10,128,128]{3,2,1,0:T(8,128)} fusion(f32[10,128,256]{2,1,0:T(8,128)S(1)} %get-tuple-element.99, bf16[256,10,128]{2,1,0:T(8,128)(2,1)S(1)} %reshape.261, f32[10,128]{1,0:T(8,128)S(1)} %get-tuple-element.97, pred[256]{0:T(512)(128)(4,1)S(1)} %reshape.258, f32[10,128]{1,0:T(8,128)S(1)} %get-tuple-element.96), kind=kOutput, calls=%fused_computation.4 | convolution fusion | flops 85032960 | bytes 2631936 | tf_op jit(solution)/shard_map/cond/branch_1_fun/vhqk,vkhd->vhqd/dot_general | solution.py:29
  69.6 26.9 %all-gather.5.cloned.1.call-done = bf16[1,512,1280]{1,2,0:T(8,128)(2,1)} async-done(((bf16[1,128,1280]{1,2,0:T(8,128)(2,1)}), bf16[1,512,1280]{1,2,0:T(8,128)(2,1)}) %all-gather.5.cloned.1.call-update) | async-done | bytes 1310736 | tf_op jit(solution)/shard_map/all_gather | solution.py:64
  96.6 5.8 %conditional.3 = (f32[1,10,128]{2,1,0:T(8,128)S(1)}, f32[1,10,128,128]{2,3,1,0:T(8,128)S(1)}) conditional(s32[]{:T(128)} %convert_element_type.31, (f32[1,10,128]{2,1,0:T(8,128)S(1)}, f32[1,10,128,128]{3,2,1,0:T(8,128)}) %tuple.22, (pred[1,128,512]{2,1,0:T(8,128)(4,1)S(1)}, bf16[1,128,10,128]{1,3,2,0:T(8,128)(2,1)S(1)}, ...), branch_computations={%region_7.8_spmd, %region_8.11_spmd} | conditional | flops 344396800 | bytes 18946092 | solution.py:41
  96.6 2.0 %fusion.13 = (f32[10,128]{1,0:T(8,128)S(1)}, f32[10,128,512]{2,1,0:T(8,128)S(1)}) fusion(pred[128,512]{1,0:T(8,128)(4,1)S(1)} %bitcast.70, bf16[512,10,128]{0,2,1:T(8,128)(2,1)} %bitcast.68, bf16[1,128,10,128]{1,3,2,0:T(8,128)(2,1)S(1)} %get-tuple-element.81), kind=kOutput, calls=%fused_computation.20 | convolution fusion | flops 169736960 | bytes 4330496 | tf_op jit(solution)/shard_map/cond/branch_1_fun/vqhd,vkhd->vhqk/dot_general | solution.py:20
  98.7 0.9 fusion.15
  99.5 0.4 copy-done.4
  100.0 2.2 %fusion.26 = f32[1,10,128,128]{3,2,1,0:T(8,128)S(1)} fusion(bf16[512,10,128]{0,2,1:T(8,128)(2,1)S(1)} %bitcast.77, f32[10,128,512]{2,1,0:T(8,128)S(1)} %get-tuple-element.95, f32[10,128]{1,0:T(8,128)S(1)} %get-tuple-element.93, pred[128,512]{1,0:T(8,128)(4,1)S(1)} %bitcast.72, f32[1,10,128,128]{3,2,1,0:T(8,128)} %get-tuple-element.42, ...), kind=kOutput, calls=%fused_computation.30 | convolution fusion | flops 171376640 | bytes 5318656 | tf_op jit(solution)/shard_map/cond/branch_1_fun/vhqk,vkhd->vhqd/dot_general | solution.py:29
  102.1 0.2 copy.58
  102.4 0.9 copy.54
  (29 shorter events, 0.6 us)
Async XLA Ops:
  6.5 4.0 %copy-start.3 = (s32[1,1,4]{2,1,0:T(1,128)S(1)}, s32[1,1,4]{2,1,0:T(1,128)}, u32[]{:S(2)}) copy-start(s32[1,1,4]{2,1,0:T(1,128)} %param.19) | copy-start | bytes 52
  6.5 8.9 %copy-start.5 = (s32[1,8]{1,0:T(1,128)S(1)}, s32[1,8]{1,0:T(1,128)}, u32[]{:S(2)}) copy-start(s32[1,8]{1,0:T(1,128)} %param.18) | copy-start | bytes 100
  6.5 8.9 %copy-start.6 = (s32[1,3]{1,0:T(1,128)S(1)}, s32[1,3]{1,0:T(1,128)}, u32[]{:S(2)}) copy-start(s32[1,3]{1,0:T(1,128)} %param.17) | copy-start | bytes 40
  6.5 10.6 %copy-start = (bf16[1,128,1280]{2,1,0:T(8,128)(2,1)S(1)}, bf16[1,128,1280]{2,1,0:T(8,128)(2,1)}, u32[]{:S(2)}) copy-start(bf16[1,128,1280]{2,1,0:T(8,128)(2,1)} %param.12) | copy-start | bytes 983044
  6.5 10.8 %copy-start.1 = (bf16[1,2,32,1280]{3,2,1,0:T(8,128)(2,1)S(1)}, bf16[1,2,32,1280]{3,2,1,0:T(8,128)(2,1)}, u32[]{:S(2)}) copy-start(bf16[1,2,32,1280]{3,2,1,0:T(8,128)(2,1)} %param.15) | copy-start | bytes 491524
  6.5 63.1 %all-gather.3.cloned.1.call-start = ((), (), s32[]{:S(2)}) async-start(), calls=%async_computation | async-start | bytes 1638400 | tf_op jit(solution)/shard_map/all_gather | solution.py:63
  8.6 36.0 %copy-start.2 = (bf16[1,2,32,1280]{3,2,1,0:T(8,128)(2,1)S(1)}, bf16[1,2,32,1280]{3,2,1,0:T(8,128)(2,1)}, u32[]{:S(2)}) copy-start(bf16[1,2,32,1280]{3,2,1,0:T(8,128)(2,1)} %param.16) | copy-start | bytes 491524
  8.6 88.0 %all-gather.5.cloned.1.call-start = ((), (), s32[]{:S(2)}) async-start(), calls=%async_computation.1 | async-start | bytes 1638400 | tf_op jit(solution)/shard_map/all_gather | solution.py:64
  98.6 1.3 %copy-start.4 = (bf16[1,512,1280]{1,2,0:T(8,128)(2,1)S(1)}, bf16[1,512,1280]{1,2,0:T(8,128)(2,1)}, u32[]{:S(2)}) copy-start(bf16[1,512,1280]{1,2,0:T(8,128)(2,1)} %get-tuple-element.43) | copy-start | bytes 3932164 | tf_op jit(solution)/shard_map/cond
Sparse Core Ops, SparseCore 0:
  8.9 54.7 all-gather.2
  65.3 31.2 all-gather.4
where the time goes:
time: 111 us; the launch traced here: 110 us
  blocking collectives  49 us (44%)
  waiting for transfers between devices  27 us (24%)
  between operations  14.9 us (13%)
  local copies, waits for them, and re-layouts  7.46 us (7%)
  matrix products  5.99 us (5%)
  other arithmetic  5.75 us (5%)
    all_gather x1, blocking collectives, body(): key_piece = lax.all_gather(cache_keys, 'seq', axis=1, tiled=True)  27.2 us
    all_gather x1, waiting for transfers between devices, body(): value_piece = lax.all_gather(values, 'seq', axis=1, tiled=True)  26.9 us
    all_gather x1, blocking collectives, body(): value_piece = lax.all_gather(cache_values, 'seq', axis=1, tiled=True)  21.8 us
    unnamed x15, local copies, waits for them, and re-layouts  4.08 us
    dot_general x2, matrix products, update(): jnp.einsum('vhqk,vkhd->vhqd', weights.astype(jnp.bfloat16), value_heads,...  3.49 us
    gather x1, other arithmetic, body(): tile_live = jnp.take(tile_mask, key_tiles, axis=2)  2.7 us
    dot_general x2, matrix products, update(): jnp.einsum('vqhd,vkhd->vhqk', query_heads, key_heads, preferred_element_t...  2.5 us
  transfers between devices with their start and end apart: 2, of which 1 were waited for; matrix products, arithmetic and copies ran while one was open for 10% of the time, Pallas kernels for 0%

commit v1 on v0

--- a/solution.py
+++ b/solution.py
@@ -52,7 +52,13 @@
     )
     frame_tok = cache_keys.shape[2]
     listed = jnp.any(frame_place[:, :, None] == frame_list[:, None, :], axis=2)
-    key_piece = lax.all_gather(cache_keys, "seq", axis=1, tiled=True)
+    peers = lax.axis_size("seq")
+    current, tiles = (cache_keys, [cache_keys])
+    for _ in range(peers - 1):
+        current = lax.ppermute(current, "seq", [(i, (i + 1) % peers) for i in range(peers)])
+        tiles.insert(0, current)
+    line = jnp.concatenate(tiles, axis=1)
+    key_piece = jnp.roll(line, (lax.axis_index("seq") + 1) * cache_keys.shape[1], axis=1)
     value_piece = lax.all_gather(cache_values, "seq", axis=1, tiled=True)
     count_frames = key_piece.shape[1]
     token_flags = jnp.repeat(listed, frame_tok, axis=1)

time: 111 us -> 107 us (0.964)
  blocking collectives: 49 us -> 22.7 us
  waiting for transfers between devices: 27 us -> 46.5 us
  starting transfers between devices: 0.08 us -> 3.22 us
    all_gather x1 -> x0, blocking collectives: 27.2 us -> none  [body(): key_piece = lax.all_gather(cache_keys, 'seq', axis=1, tiled=True)]
    ppermute x0 -> x3, waiting for transfers between devices: none -> 14.8 us  [body(): lax.ppermute(current, 'seq', [(i, (i + 1) % peers) for i in range(peers)])]
    all_gather x1, waiting for transfers between devices: 26.9 us -> 31.7 us  [body(): value_piece = lax.all_gather(values, 'seq', axis=1, tiled=True)]
    ppermute x0 -> x3, starting transfers between devices: none -> 3.14 us  [body(): lax.ppermute(current, 'seq', [(i, (i + 1) % peers) for i in range(peers)])]
    unnamed x15 -> x22, local copies, waits for them, and re-layouts: 4.08 us -> 4.17 us
  transfers between devices with their start and end apart: 2 -> 5, of which waited for: 1 -> 3; matrix products, arithmetic and copies ran while one was open for 10% -> 10% of each run, Pallas kernels for 0% -> 0%
where the time goes in v1:
time: 107 us
  waiting for transfers between devices  46.5 us (43%)
  blocking collectives  22.7 us (21%)
  between operations  15 us (14%)
  local copies, waits for them, and re-layouts  7.54 us (7%)
  matrix products  6.03 us (6%)
  other arithmetic  5.46 us (5%)
  starting transfers between devices  3.22 us (3%)
    all_gather x1, waiting for transfers between devices, body(): value_piece = lax.all_gather(values, 'seq', axis=1, tiled=True)  31.7 us
    all_gather x1, blocking collectives, body(): value_piece = lax.all_gather(cache_values, 'seq', axis=1, tiled=True)  22.7 us
    ppermute x3, waiting for transfers between devices, body(): lax.ppermute(current, 'seq', [(i, (i + 1) % peers) for i in range(peers)])  14.8 us
    unnamed x22, local copies, waits for them, and re-layouts  4.17 us
    dot_general x2, matrix products, update(): jnp.einsum('vhqk,vkhd->vhqd', weights.astype(jnp.bfloat16), value_heads,...  3.65 us
    ppermute x3, starting transfers between devices, body(): lax.ppermute(current, 'seq', [(i, (i + 1) % peers) for i in range(peers)])  3.14 us
    gather x1, other arithmetic, body(): tile_live = jnp.take(tile_mask, key_tiles, axis=2)  2.62 us
    dot_general x2, matrix products, update(): jnp.einsum('vqhd,vkhd->vhqk', query_heads, key_heads, preferred_element_t...  2.38 us
  transfers between devices with their start and end apart: 5, of which 3 were waited for; matrix products, arithmetic and copies ran while one was open for 10% of the time, Pallas kernels for 0%

profile of v1, /device:TPU:0, one launch (start us, length us, event | category | flops | bytes accessed | tf_op | source)
XLA Modules:
  0.0 106.6 jit_solution(9822175464285835835)
XLA Ops:
  6.6 2.0 %copy.49 = bf16[1,128,1280]{1,2,0:T(8,128)(2,1)} copy(bf16[1,128,1280]{2,1,0:T(8,128)(2,1)} %param.13) | data formatting | bytes 655360 | tf_op args[1]
  8.6 3.1 %collective-permute-start = (bf16[1,2,32,1280]{3,2,1,0:T(8,128)(2,1)}, bf16[1,2,32,1280]{3,2,1,0:T(8,128)(2,1)S(1)}, u32[]{:S(2)}, u32[]{:S(2)}) collective-permute-start(bf16[1,2,32,1280]{3,2,1,0:T(8,128)(2,1)} %param.15), channel_id=1, source_target_pairs={{0,4},{4,8},{8,12},{12,0},{1,5},{5,9},{9,13},{13,1},{2,6},{6,10},{... | collective-permute-start | bytes 491528 | tf_op jit(solution)/shard_map/ppermute | solution.py:58
  11.7 1.9 %copy.50 = bf16[1,128,1280]{1,2,0:T(8,128)(2,1)} copy(bf16[1,128,1280]{2,1,0:T(8,128)(2,1)} %param.14) | data formatting | bytes 655360 | tf_op args[2]
  13.6 22.7 %all_gather.9 = bf16[1,8,32,1280]{3,2,0,1:T(8,128)(2,1)S(1)} all-gather(bf16[1,2,32,1280]{3,2,0,1:T(8,128)(2,1)S(1)} %bitcast.72), channel_id=1, replica_groups=mesh['groups'=2,'seq'=4,'head'=2,'batch'=2] {'seq'}, dimensions={1}, use_global_device_ids=true | all-gather | bytes 819200 | tf_op jit(solution)/shard_map/all_gather | solution.py:62
  36.4 0.7 fusion.42
  37.1 2.6 %compare_select_fusion.1 = s32[512,1]{0,1:T(1,128)S(1)} fusion(s32[]{:T(128)} %bitcast.15, s32[]{:T(128)} %bitcast.16, s32[]{:T(128)} %bitcast.18, s32[]{:T(128)} %bitcast.17), kind=kLoop, calls=%fused_computation.55 | loop fusion | flops 8704 | bytes 2064 | tf_op jit(solution)/shard_map/jit(_take)/gather | solution.py:73
  39.9 10.6 %collective-permute-done.1 = bf16[1,2,32,1280]{3,2,1,0:T(8,128)(2,1)S(1)} collective-permute-done((bf16[1,2,32,1280]{3,2,1,0:T(8,128)(2,1)S(1)}, bf16[1,2,32,1280]{3,2,1,0:T(8,128)(2,1)S(1)}, u32[]{:S(2)}, u32[]{:S(2)}) %collective-permute-start.1) | collective-permute-done | bytes 163872 | tf_op jit(solution)/shard_map/ppermute | solution.py:58
  50.5 0.8 broadcast_reduce_fusion
  52.1 0.7 broadcast_reduce_fusion.1
  53.8 4.2 %collective-permute-done.2 = bf16[1,2,32,1280]{3,2,1,0:T(8,128)(2,1)S(1)} collective-permute-done((bf16[1,2,32,1280]{3,2,1,0:T(8,128)(2,1)S(1)}, bf16[1,2,32,1280]{3,2,1,0:T(8,128)(2,1)S(1)}, u32[]{:S(2)}, u32[]{:S(2)}) %collective-permute-start.2) | collective-permute-done | bytes 163872 | tf_op jit(solution)/shard_map/ppermute | solution.py:58
  58.2 3.1 %conditional.2 = (f32[1,10,128]{2,1,0:T(8,128)S(1)}, f32[1,10,128]{2,1,0:T(8,128)S(1)}, f32[1,10,128,128]{3,2,1,0:T(8,128)}) conditional(s32[]{:T(128)} %convert_element_type.35, () %tuple.31, (pred[8,32]{1,0:T(8,128)(4,1)S(1)}, s32[]{:T(128)}, s32[]{:T(128)}, bf16[1,16,32,1280]{3,2,1,0:T(8,128)(2,1)S(1)}, bf16[1,128,10,128]{1,3,2,0:T(8,128)(2,1)S(1)}, ...), branch_computations={%region_3.4_spmd, %region_4.7_spmd} | conditional | flops 170891536 | bytes 10220983 | solution.py:41
  58.3 0.4 reshape.285
  58.8 0.4 fusion.41
  59.1 0.3 fusion.4
  59.4 0.4 reshape.287
  59.8 1.5 %fusion.2 = f32[1,10,128,128]{3,2,1,0:T(8,128)} fusion(f32[10,128,256]{1,2,0:T(8,128)S(1)} %get-tuple-element.208, bf16[256,10,128]{2,1,0:T(8,128)(2,1)S(1)} %reshape.287, f32[10,128]{1,0:T(8,128)S(1)} %get-tuple-element.206, pred[256]{0:T(512)(128)(4,1)S(1)} %reshape.284, f32[10,128]{1,0:T(8,128)S(1)} %get-tuple-element.205), kind=kOutput, calls=%fused_computation.5 | convolution fusion | flops 85032960 | bytes 2631936 | tf_op jit(solution)/shard_map/cond/branch_1_fun/vhqk,vkhd->vhqd/dot_general | solution.py:29
  61.3 31.7 %all-gather.5.cloned.1.call-done = bf16[1,512,1280]{1,2,0:T(8,128)(2,1)} async-done(((bf16[1,128,1280]{1,2,0:T(8,128)(2,1)}), bf16[1,512,1280]{1,2,0:T(8,128)(2,1)}) %all-gather.5.cloned.1.call-update) | async-done | bytes 1310736 | tf_op jit(solution)/shard_map/all_gather | solution.py:70
  93.0 5.8 %conditional.3 = (f32[1,10,128]{2,1,0:T(8,128)S(1)}, f32[1,10,128,128]{2,3,1,0:T(8,128)S(1)}) conditional(s32[]{:T(128)} %convert_element_type.34, (f32[1,10,128]{2,1,0:T(8,128)S(1)}, f32[1,10,128,128]{3,2,1,0:T(8,128)}) %tuple.33, (pred[1,128,512]{2,1,0:T(8,128)(4,1)S(1)}, bf16[1,128,10,128]{1,3,2,0:T(8,128)(2,1)S(1)}, ...), branch_computations={%region_7.8_spmd, %region_8.11_spmd} | conditional | flops 344396800 | bytes 18946092 | solution.py:41
  93.1 2.0 %fusion.14 = (f32[10,128]{1,0:T(8,128)S(1)}, f32[10,128,512]{2,1,0:T(8,128)S(1)}) fusion(pred[128,512]{1,0:T(8,128)(4,1)S(1)} %bitcast.69, bf16[512,10,128]{0,2,1:T(8,128)(2,1)} %bitcast.67, bf16[1,128,10,128]{1,3,2,0:T(8,128)(2,1)S(1)} %get-tuple-element.188), kind=kOutput, calls=%fused_computation.22 | convolution fusion | flops 169736960 | bytes 4330496 | tf_op jit(solution)/shard_map/cond/branch_1_fun/vqhd,vkhd->vhqk/dot_general | solution.py:20
  95.1 0.9 fusion.16
  96.0 0.4 copy-done.4
  96.4 2.1 %fusion.27 = f32[1,10,128,128]{3,2,1,0:T(8,128)S(1)} fusion(bf16[512,10,128]{0,2,1:T(8,128)(2,1)S(1)} %bitcast.75, f32[10,128,512]{2,1,0:T(8,128)S(1)} %get-tuple-element.204, f32[10,128]{1,0:T(8,128)S(1)} %get-tuple-element.202, pred[128,512]{1,0:T(8,128)(4,1)S(1)} %bitcast.71, f32[1,10,128,128]{3,2,1,0:T(8,128)} %get-tuple-element.128, ...), kind=kOutput, calls=%fused_computation.32 | convolution fusion | flops 171376640 | bytes 5318656 | tf_op jit(solution)/shard_map/cond/branch_1_fun/vhqk,vkhd->vhqd/dot_general | solution.py:29
  98.6 0.2 copy.58
  98.9 0.9 copy.53
  (42 shorter events, 1.0 us)
Async XLA Ops:
  6.5 7.1 %copy-start.2 = (bf16[1,2,32,1280]{3,2,1,0:T(8,128)(2,1)S(1)}, bf16[1,2,32,1280]{3,2,1,0:T(8,128)(2,1)}, u32[]{:S(2)}) copy-start(bf16[1,2,32,1280]{3,2,1,0:T(8,128)(2,1)} %param.16) | copy-start | bytes 491524
  6.5 29.8 %copy-start.3 = (s32[1,1,4]{2,1,0:T(1,128)S(1)}, s32[1,1,4]{2,1,0:T(1,128)}, u32[]{:S(2)}) copy-start(s32[1,1,4]{2,1,0:T(1,128)} %param.19) | copy-start | bytes 52
  6.5 33.2 %copy-start.5 = (s32[1,8]{1,0:T(1,128)S(1)}, s32[1,8]{1,0:T(1,128)}, u32[]{:S(2)}) copy-start(s32[1,8]{1,0:T(1,128)} %param.18) | copy-start | bytes 100
  6.5 33.3 %copy-start.6 = (s32[1,3]{1,0:T(1,128)S(1)}, s32[1,3]{1,0:T(1,128)}, u32[]{:S(2)}) copy-start(s32[1,3]{1,0:T(1,128)} %param.17) | copy-start | bytes 40
  6.5 47.0 %copy-start.1 = (bf16[1,128,1280]{2,1,0:T(8,128)(2,1)S(1)}, bf16[1,128,1280]{2,1,0:T(8,128)(2,1)}, u32[]{:S(2)}) copy-start(bf16[1,128,1280]{2,1,0:T(8,128)(2,1)} %param.12) | copy-start | bytes 983044
  6.5 54.8 %all-gather.3.cloned.1.call-start = ((), (), s32[]{:S(2)}) async-start(), calls=%async_computation | async-start | bytes 1638400 | tf_op jit(solution)/shard_map/all_gather | solution.py:69
  8.6 84.4 %all-gather.5.cloned.1.call-start = ((), (), s32[]{:S(2)}) async-start(), calls=%async_computation.1 | async-start | bytes 1638400 | tf_op jit(solution)/shard_map/all_gather | solution.py:70
  8.6 31.0 %collective-permute-start = (bf16[1,2,32,1280]{3,2,1,0:T(8,128)(2,1)}, bf16[1,2,32,1280]{3,2,1,0:T(8,128)(2,1)S(1)}, u32[]{:S(2)}, u32[]{:S(2)}) collective-permute-start(bf16[1,2,32,1280]{3,2,1,0:T(8,128)(2,1)} %param.15), channel_id=1, source_target_pairs={{0,4},{4,8},{8,12},{12,0},{1,5},{5,9},{9,13},{13,1},{2,6},{6,10},{... | collective-permute-start | bytes 491528 | tf_op jit(solution)/shard_map/ppermute | solution.py:58
  13.6 44.4 %copy-start = (bf16[1,2,32,1280]{3,2,1,0:T(8,128)(2,1)S(1)}, bf16[1,2,32,1280]{3,2,1,0:T(8,128)(2,1)}, u32[]{:S(2)}) copy-start(bf16[1,2,32,1280]{3,2,1,0:T(8,128)(2,1)} %param.15) | copy-start | bytes 491524
  39.7 10.8 %collective-permute-start.1 = (bf16[1,2,32,1280]{3,2,1,0:T(8,128)(2,1)S(1)}, bf16[1,2,32,1280]{3,2,1,0:T(8,128)(2,1)S(1)}, u32[]{:S(2)}, u32[]{:S(2)}) collective-permute-start(bf16[1,2,32,1280]{3,2,1,0:T(8,128)(2,1)S(1)} %collective-permute-done), channel_id=1, source_target_pairs={{0,4},{4,8},{8,12},{12,0},{1,5},{5,9},{9,13},{13,1},{2,6},{6,10},{... | collective-permute-start | bytes 491528 | tf_op jit(solution)/shard_map/ppermute | solution.py:58
  50.5 7.5 %collective-permute-start.2 = (bf16[1,2,32,1280]{3,2,1,0:T(8,128)(2,1)S(1)}, bf16[1,2,32,1280]{3,2,1,0:T(8,128)(2,1)S(1)}, u32[]{:S(2)}, u32[]{:S(2)}) collective-permute-start(bf16[1,2,32,1280]{3,2,1,0:T(8,128)(2,1)S(1)} %collective-permute-done.1), channel_id=1, source_target_pairs={{0,4},{4,8},{8,12},{12,0},{1,5},{5,9},{9,13},{13,1},{2,6},{6,10},{... | collective-permute-start | bytes 491528 | tf_op jit(solution)/shard_map/ppermute | solution.py:58
  95.1 1.3 %copy-start.4 = (bf16[1,512,1280]{1,2,0:T(8,128)(2,1)S(1)}, bf16[1,512,1280]{1,2,0:T(8,128)(2,1)}, u32[]{:S(2)}) copy-start(bf16[1,512,1280]{1,2,0:T(8,128)(2,1)} %get-tuple-element.129) | copy-start | bytes 3932164 | tf_op jit(solution)/shard_map/cond
Sparse Core Ops, SparseCore 0:
  8.9 47.7 all-gather.2
  58.3 34.6 all-gather.4
